TPU v7x, 512 devices: a whole 4x4x16 slice. The times are simulated.
512 devices in a mesh: dp: 32 (over y, x, core), fsdp: 16 (over z).
Axes of the slice: x: 4, y: 4, z: 16, core: 2. Of those that a mesh axis runs over, the one named last changes fastest.
Arguments:
- queries: bfloat16 [131072, 2048], P(('dp', 'fsdp')), may hold values from -600 to 600
- w_kv: bfloat16 [2, 2048, 896], P(None, 'fsdp'), may hold values from -0.1875 to 0.1875
- encodings: bfloat16 [196608, 896], P(('dp', 'fsdp')), may hold values from -6 to 6
- counts: int32 [512], P(('dp', 'fsdp')), may hold values from 48 to 384, as said below
- owner_rank: int32 [196608], P(('dp', 'fsdp')), may hold values from 0 to 31, as said below
- owner_span: int32 [196608], P(('dp', 'fsdp')), may hold values from 0 to 3, as said below
- grad_ctx: bfloat16 [131072, 2048], P(('dp', 'fsdp')), may hold values from -24 to 24
Outputs:
- grad_queries: bfloat16 [131072, 2048], P(('dp', 'fsdp'))
- grad_value: bfloat16 [2048, 896], P('fsdp')
Inputs may be any that keep to these rules, and one draw needn't show every extreme that they name: `counts`: each count is 384 divided by 1, 2, 4 or 8; among the devices of equal fsdp index one holds 384. `owner_rank`: among the live rows of one device at most 12 name the same owner; a device whose count is 384 names every owner exactly 12 times. `owner_span`: every span of every decoder device is named by at least one live row of a device with equal fsdp index.
All inputs are finite; a program needn't handle non-finite values.
Results may differ from a plain program's by a relative error of at most 0.023.
Values may be sent and summed in bfloat16 or wider, within the bound.
No kernel may reach another device: no remote copies, remote signals or barrier semaphores. Data moves between devices by JAX's collectives and lax.ppermute only.
A program may use at most 64 MiB of HBM per device.

v0:
```python
import jax
import jax.numpy as jnp
from jax import lax
from jax.sharding import PartitionSpec as P

HEADS = 16
HEAD_DIM = 128
SPAN = 64


def total_of_pieces(array, axis):
    return lax.all_gather(array, axis).astype(jnp.float32).sum(0)


def pack_rows(enc_rows, live_count, rank_rows, span_rows, dp_count):
    row_total = enc_rows.shape[0]
    pair_slots = row_total // dp_count
    live_rows = jnp.arange(row_total, dtype=jnp.int32) < live_count
    hit_table = (
        (rank_rows[:, None] == jnp.arange(dp_count, dtype=jnp.int32)[None, :]) & live_rows[:, None]
    ).astype(jnp.int32)
    before_hits = jnp.cumsum(hit_table, axis=0) - hit_table
    slot_index = jnp.sum(before_hits * hit_table, axis=1)
    target = jnp.where(live_rows, rank_rows * pair_slots + slot_index, dp_count * pair_slots)
    buffer = (
        jnp.zeros((dp_count * pair_slots, enc_rows.shape[1]), enc_rows.dtype)
        .at[target]
        .set(enc_rows, mode="drop")
    )
    tag_buffer = (
        jnp.full((dp_count * pair_slots,), -1, jnp.int32).at[target].set(span_rows, mode="drop")
    )
    return (
        buffer.reshape(dp_count, pair_slots, enc_rows.shape[1]),
        tag_buffer.reshape(dp_count, pair_slots),
    )


def local(queries, w_kv, encodings, counts, owner_rank, owner_span, grad_ctx):
    dp_count = lax.axis_size("dp")
    slot_total = encodings.shape[0]
    width = encodings.shape[1]
    buffer, tag_buffer = pack_rows(encodings, counts[0], owner_rank, owner_span, dp_count)
    arrived, arrived_tags = (
        lax.all_to_all(buffer, "dp", split_axis=0, concat_axis=0, tiled=True),
        lax.all_to_all(tag_buffer, "dp", split_axis=0, concat_axis=0, tiled=True),
    )
    received = arrived.reshape(slot_total, width)
    tag_rows = arrived_tags.reshape(slot_total)
    projected = jnp.einsum(
        "re,kne->krn",
        received,
        lax.all_gather(w_kv, "fsdp", axis=1, tiled=True),
        preferred_element_type=jnp.float32,
    ).astype(jnp.bfloat16)
    keys = projected[0]
    values = projected[1]
    token_total = queries.shape[0]
    scale = 1.0 / HEAD_DIM**0.5
    query_heads = queries.reshape(token_total, HEADS, HEAD_DIM)
    key_heads = keys.reshape(slot_total, HEADS, HEAD_DIM)
    value_heads = values.reshape(slot_total, HEADS, HEAD_DIM)
    grad_heads = grad_ctx.reshape(token_total, HEADS, HEAD_DIM)
    scores = (
        jnp.einsum("thd,khd->htk", query_heads, key_heads, preferred_element_type=jnp.float32)
        * scale
    )
    token_span = jnp.arange(token_total, dtype=jnp.int32) // SPAN
    allowed = (token_span[:, None] == tag_rows[None, :])[None]
    masked = jnp.where(allowed, scores, -1e30)
    highest = jnp.max(masked, axis=-1, keepdims=True)
    weights = jnp.where(allowed, jnp.exp(masked - highest), 0.0)
    probs = weights / jnp.sum(weights, axis=-1, keepdims=True)
    probs_low = probs.astype(jnp.bfloat16)
    context = jnp.einsum("htk,khd->thd", probs_low, value_heads, preferred_element_type=jnp.float32)
    dprob = jnp.einsum("thd,khd->htk", grad_heads, value_heads, preferred_element_type=jnp.float32)
    delta = jnp.transpose(jnp.sum(grad_heads.astype(jnp.float32) * context, axis=-1))[:, :, None]
    dscore = (probs * (dprob - delta)).astype(jnp.bfloat16)
    grad_query = (
        jnp.einsum("htk,khd->thd", dscore, key_heads, preferred_element_type=jnp.float32) * scale
    )
    grad_queries = grad_query.astype(jnp.bfloat16).reshape(token_total, HEADS * HEAD_DIM)
    dval = jnp.einsum("htk,thd->khd", probs_low, grad_heads, preferred_element_type=jnp.float32)
    dval = dval.astype(jnp.bfloat16).reshape(slot_total, HEADS * HEAD_DIM)
    shard_sum = lax.psum_scatter(
        lax.dot_general(
            dval, received, (((0,), (0,)), ((), ())), preferred_element_type=jnp.float32
        ).astype(jnp.bfloat16),
        "fsdp",
        scatter_dimension=0,
        tiled=True,
    )
    group_sum = total_of_pieces(shard_sum, "dp").astype(jnp.float32)
    grad_value = (group_sum / dp_count).astype(jnp.bfloat16)
    return (grad_queries, grad_value)


def solution(mesh):
    in_specs = (
        P(("dp", "fsdp"), None),
        P(None, "fsdp", None),
        P(("dp", "fsdp"), None),
        P(("dp", "fsdp")),
        P(("dp", "fsdp")),
        P(("dp", "fsdp")),
        P(("dp", "fsdp"), None),
    )
    out_specs = (P(("dp", "fsdp"), None), P("fsdp", None))
    return jax.shard_map(local, mesh=mesh, in_specs=in_specs, out_specs=out_specs, check_vma=False)
```

profile of v0, /device:TPU:1, one launch (start us, length us, event | category | flops | bytes accessed | tf_op | source)
XLA Modules:
  0.0 291.8 jit_solution(403865007647869411)
XLA Ops:
  8.6 0.7 fusion.26
  9.3 0.9 reduce-window.6
  10.4 0.8 fusion.23
  11.9 3.1 %scatter_custom_fusion.1 = s32[384]{0:T(512)S(1)} fusion(s32[384]{0:T(512)S(1)} %compare_select_fusion, s32[384]{0:T(512)} %param.12, s32[]{:T(128)} %constant.40.clone.1), kind=kCustom, calls=%fused_computation.49 | custom fusion | bytes 2048 | tf_op jit(solution)/shard_map/scatter | solution.py:31
  15.0 0.7 all_to_all.10
  15.7 10.3 %all-to-all-start.1 = ((s32[32,1,12]{2,1,0:T(1,128)}), s32[32,1,12]{2,1,0:T(1,128)S(1)}, u32[]{:S(2)}, u32[]{:S(2)}) async-start(s32[32,1,12]{2,1,0:T(1,128)} %bitcast.4), calls=%async_computation.1 | async-start | bytes 32768 | tf_op jit(solution)/shard_map/all_to_all | solution.py:46
  26.0 2.9 scatter_custom_fusion
  28.9 1.1 reshape.101
  30.0 3.0 %all-to-all-done.1 = s32[32,1,12]{2,1,0:T(1,128)S(1)} async-done(((s32[32,1,12]{2,1,0:T(1,128)}), s32[32,1,12]{2,1,0:T(1,128)S(1)}, u32[]{:S(2)}, u32[]{:S(2)}) %all-to-all-start.1) | async-done | bytes 1568 | tf_op jit(solution)/shard_map/all_to_all | solution.py:46
  33.0 4.5 %all-to-all-start = ((bf16[32,12,896]{2,1,0:T(8,128)(2,1)}), bf16[32,12,896]{2,1,0:T(8,128)(2,1)S(1)}, u32[]{:S(2)}, u32[]{:S(2)}) async-start(bf16[32,12,896]{2,1,0:T(8,128)(2,1)} %reshape.101), calls=%async_computation | async-start | bytes 1835008 | tf_op jit(solution)/shard_map/all_to_all | solution.py:45
  37.7 1.3 copy.28
  40.5 12.6 %all-to-all-done = bf16[32,12,896]{2,1,0:T(8,128)(2,1)S(1)} async-done(((bf16[32,12,896]{2,1,0:T(8,128)(2,1)}), bf16[32,12,896]{2,1,0:T(8,128)(2,1)S(1)}, u32[]{:S(2)}, u32[]{:S(2)}) %all-to-all-start) | async-done | bytes 688160 | tf_op jit(solution)/shard_map/all_to_all | solution.py:45
  53.1 1.0 reshape.127
  54.3 56.3 %all-gather.4.cloned.1.call-done = bf16[2,2048,896]{2,1,0:T(8,128)(2,1)} async-done(((bf16[2,128,896]{2,1,0:T(8,128)(2,1)}), bf16[2,2048,896]{2,1,0:T(8,128)(2,1)}) %all-gather.4.cloned.1.call-update) | async-done | bytes 7340048 | tf_op jit(solution)/shard_map/all_gather | solution.py:53
  110.6 6.8 %fusion.9 = bf16[2,384,2048]{2,1,0:T(8,128)(2,1)S(1)} fusion(bf16[384,896,1]{1,0,2:T(8,128)(2,1)} %reshape.127, bf16[2,2048,896]{2,1,0:T(8,128)(2,1)} %all-gather.4.cloned.1.call-done), kind=kOutput, calls=%fused_computation.17 | convolution fusion | flops 2820145152 | bytes 11173888 | tf_op jit(solution)/shard_map/re,kne->krn/dot_general | solution.py:50
  117.4 1.5 fusion.31
  118.8 2.6 copy.45
  121.4 2.4 fusion.16
  123.9 2.5 fusion.32
  126.4 0.7 fusion.12
  127.1 1.9 copy-done.2
  129.1 1.6 copy-done.1
  130.7 1.0 convolution_convert_fusion.2
  131.7 4.0 %convolution_convert_fusion = bf16[2048,896]{1,0:T(8,128)(2,1)} fusion(bf16[384,2048]{0,1:T(8,128)(2,1)S(1)} %bitcast.90, bf16[384,896]{1,0:T(8,128)(2,1)S(1)} %reshape.102), kind=kOutput, calls=%fused_computation.9 | convolution fusion | flops 1411121152 | bytes 5931008 | tf_op jit(solution)/shard_map/dot_general | solution.py:86
  136.0 67.2 %reduce-scatter.2.cloned.1.call-done = bf16[128,896]{1,0:T(8,128)(2,1)} async-done(((bf16[2048,896]{1,0:T(8,128)(2,1)}), bf16[128,896]{1,0:T(8,128)(2,1)}) %reduce-scatter.2.cloned.1.call-update) | async-done | bytes 229392 | tf_op jit(solution)/shard_map/reduce_scatter | solution.py:85
  203.3 1.6 copy.46
  204.9 3.5 %fusion.13 = f32[256,16]{0,1:T(8,128)S(1)} fusion(bf16[256,16,128]{0,2,1:T(8,128)(2,1)} %bitcast.85, bf16[384,16,128]{0,2,1:T(8,128)(2,1)} %bitcast.88, bf16[16,256,384]{1,2,0:T(8,128)(2,1)} %copy-done.1), kind=kOutput, calls=%fused_computation.21 | convolution fusion | flops 404221952 | bytes 5783552 | tf_op jit(solution)/shard_map/htk,khd->thd/dot_general | solution.py:75
  208.4 6.5 %multiply_convert_fusion = bf16[16,128,256]{2,1,0:T(8,128)(2,1)} fusion(bf16[384,16,128]{0,2,1:T(8,128)(2,1)S(1)} %bitcast.84, f32[16,256]{1,0:T(8,128)S(1)} %bitcast.94, bf16[384,16,128]{0,2,1:T(8,128)(2,1)} %bitcast.89, bf16[256,16,128]{0,2,1:T(8,128)(2,1)} %bitcast.86, f32[16,256,384]{1,2,0:T(8,128)} %copy-done.2, f32[16,256]{1,0:T(8,128)S(1)} %get-tuple-element.10), kind=kOutput, calls=%fused_computation.22 | convolution fusion | flops 812646400 | bytes 11567104 | tf_op jit(solution)/shard_map/htk,khd->thd/dot_general | solution.py:80
  214.9 2.3 copy.38
  217.1 63.3 %all-gather.6.cloned.1.call-done = bf16[4096,896]{1,0:T(8,128)(2,1)} async-done(((bf16[128,896]{1,0:T(8,128)(2,1)}), bf16[4096,896]{1,0:T(8,128)(2,1)}) %all-gather.6.cloned.1.call-update) | async-done | bytes 7340048 | tf_op jit(solution)/shard_map/all_gather | solution.py:12
  280.4 4.2 %convert_reduce_fusion = f32[128,896]{1,0:T(8,128)S(1)} fusion(bf16[32,128,896]{2,1,0:T(8,128)(2,1)} %bitcast.82), kind=kLoop, calls=%fused_computation.3 | loop fusion | flops 7225344 | bytes 7798784 | tf_op jit(solution)/shard_map/reduce_sum | solution.py:12
  284.5 0.7 multiply_convert_fusion.1
  (27 shorter events, 3.8 us)
Async XLA Ops:
  7.2 114.3 %copy-start = (bf16[256,2048]{1,0:T(8,128)(2,1)S(1)}, bf16[256,2048]{1,0:T(8,128)(2,1)}, u32[]{:S(2)}) copy-start(bf16[256,2048]{1,0:T(8,128)(2,1)} %param.7) | copy-start | bytes 3145732
  7.2 30.6 %copy-start.5 = (bf16[256,2048]{1,0:T(8,128)(2,1)S(1)}, bf16[256,2048]{1,0:T(8,128)(2,1)}, u32[]{:S(2)}) copy-start(bf16[256,2048]{1,0:T(8,128)(2,1)} %param.13) | copy-start | bytes 3145732
  7.2 103.4 %all-gather.4.cloned.1.call-start = ((), (), s32[]{:S(2)}) async-start(), calls=%async_computation.3 | async-start | bytes 7798784 | tf_op jit(solution)/shard_map/all_gather | solution.py:53
  15.7 17.3 %all-to-all-start.1 = ((s32[32,1,12]{2,1,0:T(1,128)}), s32[32,1,12]{2,1,0:T(1,128)S(1)}, u32[]{:S(2)}, u32[]{:S(2)}) async-start(s32[32,1,12]{2,1,0:T(1,128)} %bitcast.4), calls=%async_computation.1 | async-start | bytes 32768 | tf_op jit(solution)/shard_map/all_to_all | solution.py:46
  33.0 20.1 %all-to-all-start = ((bf16[32,12,896]{2,1,0:T(8,128)(2,1)}), bf16[32,12,896]{2,1,0:T(8,128)(2,1)S(1)}, u32[]{:S(2)}, u32[]{:S(2)}) async-start(bf16[32,12,896]{2,1,0:T(8,128)(2,1)} %reshape.101), calls=%async_computation | async-start | bytes 1835008 | tf_op jit(solution)/shard_map/all_to_all | solution.py:45
  37.5 165.8 %reduce-scatter.2.cloned.1.call-start = ((), (), s32[]{:S(2)}) async-start(), calls=%async_computation.4 | async-start | bytes 3899392 | tf_op jit(solution)/shard_map/reduce_scatter | solution.py:85
  126.4 2.7 copy-start.2
  126.4 4.3 %copy-start.4 = (bf16[256,2048]{0,1:T(8,128)(2,1)S(1)}, bf16[256,2048]{0,1:T(8,128)(2,1)}, u32[]{:S(2)}) copy-start(bf16[256,2048]{0,1:T(8,128)(2,1)} %copy.28) | copy-start | bytes 3145732
  129.1 1.6 copy-start.1
  135.8 144.6 %all-gather.6.cloned.1.call-start = ((), (), s32[]{:S(2)}) async-start(), calls=%async_computation.5 | async-start | bytes 7569408 | tf_op jit(solution)/shard_map/all_gather | solution.py:12
  204.9 3.5 %copy-start.3 = (bf16[1,384,2048]{1,2,0:T(8,128)(2,1)S(1)}, bf16[1,384,2048]{1,2,0:T(8,128)(2,1)}, u32[]{:S(2)}) copy-start(bf16[1,384,2048]{1,2,0:T(8,128)(2,1)} %copy.45) | copy-start | bytes 4718596
Sparse Core Ops, SparseCore 0:
  10.1 100.4 all-gather.3
  135.9 67.3 reduce-scatter.1
  206.4 73.9 all-gather.5
where the time goes:
time: 292 us
  waiting for transfers between devices  203 us (70%)
  matrix products  24.1 us (8%)
  local copies, waits for them, and re-layouts  22.6 us (8%)
  starting transfers between devices  15.3 us (5%)
  between operations  14.6 us (5%)
  other arithmetic  12 us (4%)
    reduce_scatter x1, waiting for transfers between devices, local(): lax.psum_scatter(lax.dot_general(dval, received, (((0,), (0,)), ((), ()))...  67.2 us
    all_gather x1, waiting for transfers between devices, total_of_pieces(): return lax.all_gather(array, axis).astype(jnp.float32).sum(0)  63.3 us
    all_gather x1, waiting for transfers between devices, local(): lax.all_gather(w_kv, 'fsdp', axis=1, tiled=True)  56.3 us
    all_to_all x1, waiting for transfers between devices, local(): lax.all_to_all(buffer, 'dp', split_axis=0, concat_axis=0, tiled=True)  12.6 us
    all_to_all x1, starting transfers between devices, local(): lax.all_to_all(tag_buffer, 'dp', split_axis=0, concat_axis=0, tiled=True)  10.3 us
    unnamed x14, local copies, waits for them, and re-layouts  7.19 us
    dot_general x1, matrix products, local(): jnp.einsum('re,kne->krn', received, lax.all_gather(w_kv, 'fsdp', axis=1,...  6.76 us
    dot_general x1, matrix products, local(): jnp.einsum('htk,khd->thd', dscore, key_heads, preferred_element_type=jnp....  6.48 us
  transfers between devices with their start and end apart: 5, of which 5 were waited for; matrix products, arithmetic and copies ran while one was open for 10% of the time, Pallas kernels for 0%

commit v1 on v0

--- a/solution.py
+++ b/solution.py
@@ -50,7 +50,9 @@
     projected = jnp.einsum(
         "re,kne->krn",
         received,
-        lax.all_gather(w_kv, "fsdp", axis=1, tiled=True),
+        jnp.concatenate(
+            lax.all_to_all(jnp.stack([w_kv] * lax.axis_size("fsdp")), "fsdp", 0, 0), axis=1
+        ),
         preferred_element_type=jnp.float32,
     ).astype(jnp.bfloat16)
     keys = projected[0]

time: 292 us -> 570 us (1.95)
  waiting for transfers between devices: 203 us -> 448 us
  blocking collectives: 0 us -> 19.4 us
  starting transfers between devices: 15.3 us -> 24 us
  local copies, waits for them, and re-layouts: 22.6 us -> 29.9 us
    all_to_all x1, waiting for transfers between devices: 12.6 us -> 312 us  [local(): lax.all_to_all(jnp.stack([w_kv] * lax.axis_size('fsdp')), 'fsdp', 0, 0)]
    all_gather x1 -> x0, waiting for transfers between devices: 56.3 us -> none  [local(): lax.all_gather(w_kv, 'fsdp', axis=1, tiled=True)]
    all_to_all x0 -> x1, blocking collectives: none -> 19.4 us  [local(): lax.all_to_all(buffer, 'dp', split_axis=0, concat_axis=0, tiled=True)]
    all_to_all x1, starting transfers between devices: 4.48 us -> 13.2 us  [local(): lax.all_to_all(jnp.stack([w_kv] * lax.axis_size('fsdp')), 'fsdp', 0, 0)]
  transfers between devices with their start and end apart: 5 -> 4, of which waited for: 5 -> 4; matrix products, arithmetic and copies ran while one was open for 10% -> 4% of each run, Pallas kernels for 0% -> 0%
where the time goes in v1:
time: 570 us; the launch traced here: 569 us
  waiting for transfers between devices  448 us (79%)
  local copies, waits for them, and re-layouts  29.9 us (5%)
  starting transfers between devices  24 us (4%)
  matrix products  20.5 us (4%)
  blocking collectives  19.4 us (3%)
  between operations  15 us (3%)
  other arithmetic  12.1 us (2%)
    all_to_all x1, waiting for transfers between devices, local(): lax.all_to_all(jnp.stack([w_kv] * lax.axis_size('fsdp')), 'fsdp', 0, 0)  312 us
    reduce_scatter x1, waiting for transfers between devices, local(): lax.psum_scatter(lax.dot_general(dval, received, (((0,), (0,)), ((), ()))...  68.1 us
    all_gather x1, waiting for transfers between devices, total_of_pieces(): return lax.all_gather(array, axis).astype(jnp.float32).sum(0)  63.8 us
    all_to_all x1, blocking collectives, local(): lax.all_to_all(buffer, 'dp', split_axis=0, concat_axis=0, tiled=True)  19.4 us
    all_to_all x1, starting transfers between devices, local(): lax.all_to_all(jnp.stack([w_kv] * lax.axis_size('fsdp')), 'fsdp', 0, 0)  13.2 us
  transfers between devices with their start and end apart: 4, of which 4 were waited for; matrix products, arithmetic and copies ran while one was open for 4% of the time, Pallas kernels for 0%

profile of v1, /device:TPU:1, one launch (start us, length us, event | category | flops | bytes accessed | tf_op | source)
XLA Modules:
  0.0 569.2 jit_solution(12969901780030397876)
XLA Ops:
  8.7 0.9 reduce-window.6
  9.8 0.8 fusion.23
  11.3 3.1 scatter_custom_fusion.1
  14.4 0.7 all_to_all.14
  15.1 10.3 %all-to-all-start.2 = ((s32[32,1,12]{2,1,0:T(1,128)}), s32[32,1,12]{2,1,0:T(1,128)S(1)}, u32[]{:S(2)}, u32[]{:S(2)}) async-start(s32[32,1,12]{2,1,0:T(1,128)} %bitcast.6), calls=%async_computation.2 | async-start | bytes 32768 | tf_op jit(solution)/shard_map/all_to_all | solution.py:46
  25.4 2.9 scatter_custom_fusion
  28.5 3.9 all-to-all-done.2
  32.4 19.4 %all_to_all.19 = bf16[32,12,896]{2,1,0:T(8,128)(2,1)S(1)} all-to-all(bf16[32,12,896]{2,1,0:T(8,128)(2,1)S(1)} %reshape.109), channel_id=1, replica_groups=mesh['dp'=32,'fsdp'=16] {'dp'}, dimensions={0} | all-to-all | bytes 1376256 | tf_op jit(solution)/shard_map/all_to_all | solution.py:45
  51.8 4.1 stack.2
  55.8 13.2 %all-to-all-start.1 = ((bf16[16,2,128,896]{3,2,1,0:T(8,128)(2,1)}), bf16[16,2,128,896]{3,2,1,0:T(8,128)(2,1)}, u32[]{:S(2)}, u32[]{:S(2)}) async-start(bf16[16,2,128,896]{3,2,1,0:T(8,128)(2,1)} %stack.2), calls=%async_computation.1 | async-start | bytes 14680064 | tf_op jit(solution)/shard_map/all_to_all | solution.py:54
  69.3 1.3 copy.29
  72.1 1.0 reshape.137
  73.3 312.5 %all-to-all-done.1 = bf16[16,2,128,896]{3,2,1,0:T(8,128)(2,1)} async-done(((bf16[16,2,128,896]{3,2,1,0:T(8,128)(2,1)}), bf16[16,2,128,896]{3,2,1,0:T(8,128)(2,1)}, u32[]{:S(2)}, u32[]{:S(2)}) %all-to-all-start.1) | async-done | bytes 7340064 | tf_op jit(solution)/shard_map/all_to_all | solution.py:54
  385.8 4.1 copy.25
  389.9 3.7 fusion.9
  393.6 1.5 fusion.31
  395.0 2.6 copy.46
  397.6 2.4 fusion.16
  400.1 2.5 fusion.32
  402.6 0.7 fusion.12
  403.3 1.9 copy-done.3
  405.3 1.6 copy-done.2
  406.9 1.0 convolution_convert_fusion.2
  407.9 4.0 convolution_convert_fusion
  412.2 68.1 %reduce-scatter.2.cloned.1.call-done = bf16[128,896]{1,0:T(8,128)(2,1)} async-done(((bf16[2048,896]{1,0:T(8,128)(2,1)}), bf16[128,896]{1,0:T(8,128)(2,1)}) %reduce-scatter.2.cloned.1.call-update) | async-done | bytes 229392 | tf_op jit(solution)/shard_map/reduce_scatter | solution.py:87
  480.3 1.6 copy.47
  481.9 3.2 fusion.13
  485.1 6.2 %multiply_convert_fusion = bf16[16,128,256]{2,1,0:T(8,128)(2,1)} fusion(bf16[384,16,128]{0,2,1:T(8,128)(2,1)S(1)} %bitcast.87, f32[16,256]{1,0:T(8,128)S(1)} %bitcast.97, bf16[384,16,128]{0,2,1:T(8,128)(2,1)} %bitcast.92, bf16[256,16,128]{0,2,1:T(8,128)(2,1)S(1)} %bitcast.90, f32[16,256,384]{1,2,0:T(8,128)} %copy-done.3, f32[16,256]{1,0:T(8,128)S(1)} %get-tuple-element.10), kind=kOutput, calls=%fused_computation.22 | convolution fusion | flops 812646400 | bytes 11567104 | tf_op jit(solution)/shard_map/htk,khd->thd/dot_general | solution.py:82
  491.3 2.3 copy.39
  493.6 63.8 %all-gather.3.cloned.1.call-done = bf16[4096,896]{1,0:T(8,128)(2,1)} async-done(((bf16[128,896]{1,0:T(8,128)(2,1)}), bf16[4096,896]{1,0:T(8,128)(2,1)}) %all-gather.3.cloned.1.call-update) | async-done | bytes 7340048 | tf_op jit(solution)/shard_map/all_gather | solution.py:12
  557.4 4.2 convert_reduce_fusion
  561.6 0.7 multiply_convert_fusion.1
  (33 shorter events, 3.9 us)
Async XLA Ops:
  7.2 390.5 %copy-start = (bf16[256,2048]{1,0:T(8,128)(2,1)S(1)}, bf16[256,2048]{1,0:T(8,128)(2,1)}, u32[]{:S(2)}) copy-start(bf16[256,2048]{1,0:T(8,128)(2,1)} %param.7) | copy-start | bytes 3145732
  7.2 44.6 %copy-start.8 = (bf16[2,128,896]{2,1,0:T(8,128)(2,1)S(1)}, bf16[2,128,896]{2,1,0:T(8,128)(2,1)}, u32[]{:S(2)}) copy-start(bf16[2,128,896]{2,1,0:T(8,128)(2,1)} %param.8) | copy-start | bytes 1376260
  15.1 17.3 %all-to-all-start.2 = ((s32[32,1,12]{2,1,0:T(1,128)}), s32[32,1,12]{2,1,0:T(1,128)S(1)}, u32[]{:S(2)}, u32[]{:S(2)}) async-start(s32[32,1,12]{2,1,0:T(1,128)} %bitcast.6), calls=%async_computation.2 | async-start | bytes 32768 | tf_op jit(solution)/shard_map/all_to_all | solution.py:46
  55.8 13.5 %copy-start.6 = (bf16[256,2048]{1,0:T(8,128)(2,1)S(1)}, bf16[256,2048]{1,0:T(8,128)(2,1)}, u32[]{:S(2)}) copy-start(bf16[256,2048]{1,0:T(8,128)(2,1)} %param.13) | copy-start | bytes 3145732
  55.8 329.9 %all-to-all-start.1 = ((bf16[16,2,128,896]{3,2,1,0:T(8,128)(2,1)}), bf16[16,2,128,896]{3,2,1,0:T(8,128)(2,1)}, u32[]{:S(2)}, u32[]{:S(2)}) async-start(bf16[16,2,128,896]{3,2,1,0:T(8,128)(2,1)} %stack.2), calls=%async_computation.1 | async-start | bytes 14680064 | tf_op jit(solution)/shard_map/all_to_all | solution.py:54
  69.1 411.2 %reduce-scatter.2.cloned.1.call-start = ((), (), s32[]{:S(2)}) async-start(), calls=%async_computation.4 | async-start | bytes 3899392 | tf_op jit(solution)/shard_map/reduce_scatter | solution.py:87
  385.8 4.1 copy-start.7
  402.6 2.7 copy-start.3
  402.6 4.3 copy-start.5
  405.3 1.6 copy-start.2
  412.0 145.4 %all-gather.3.cloned.1.call-start = ((), (), s32[]{:S(2)}) async-start(), calls=%async_computation.5 | async-start | bytes 7569408 | tf_op jit(solution)/shard_map/all_gather | solution.py:12
  481.9 3.2 copy-start.4
  557.4 5.0 copy-start.1
Sparse Core Ops, SparseCore 0:
  412.1 68.1 reduce-scatter.1
  483.4 73.8 all-gather.2
